TPU v7x, 32 devices: a whole 2x2x4 slice. The times are simulated.
32 devices in a mesh: occ: 16 (over z, y, core), vir: 2 (over x).
Axes of the slice: x: 2, y: 2, z: 4, core: 2. Of those that a mesh axis runs over, the one named last changes fastest.
Arguments:
- lambda_triples: bfloat16 [256, 320, 320], P('occ', 'vir'), may hold values from -6 to 6
- amplitude_triples: bfloat16 [256, 320, 320], P('occ', 'vir'), may hold values from -6 to 6
- spin_extent: int32 [256], P('occ'), may hold values from 80 to 320
- ladder_weight: bfloat16 [320, 320], P(None, 'vir'), may hold values from -0.3125 to 0.3125
- cycle_weight: bfloat16 [320, 40], replicated, may hold values from -0.3125 to 0.3125
- lambda_doubles: bfloat16 [40, 320], P(None, 'vir'), may hold values from -1 to 1
Outputs:
- residual: bfloat16 [256, 320, 320], P('occ', 'vir')
All inputs are finite; a program needn't handle non-finite values.
Results may differ from a plain program's by a relative error of at most 0.0043.
Values may be sent and summed in bfloat16 or wider, within the bound.
No kernel may reach another device: no remote copies, remote signals or barrier semaphores. Data moves between devices by JAX's collectives and lax.ppermute only.
A program may use at most 64 MiB of HBM per device.

v0:
```python
import jax
import jax.numpy as jnp
from jax import lax
from jax.sharding import PartitionSpec as P


def on_device(
    lambda_triples, amplitude_triples, spin_extent, ladder_weight, cycle_weight, lambda_doubles
):
    f32 = jnp.float32
    width = lambda_triples.shape[2]
    triples_all = lambda_triples.shape[0] * lax.axis_size("occ")
    columns = jnp.arange(width, dtype=jnp.int32)
    keep = columns[None, :] < spin_extent[:, None]
    masked = jnp.where(keep[:, None, :], lambda_triples, jnp.zeros_like(lambda_triples))
    ladder_full, doubles_full = (
        lax.all_gather(ladder_weight, "vir", axis=1, tiled=True),
        lax.all_gather(lambda_doubles, "vir", axis=1, tiled=True),
    )
    ladder_term = jnp.einsum("tae,eb->tab", masked, ladder_full, preferred_element_type=f32)
    cycle_mid = jnp.einsum(
        "tae,em->tam", amplitude_triples, cycle_weight, preferred_element_type=f32
    ).astype(jnp.bfloat16)
    cycle_term = jnp.einsum("tam,mb->tab", cycle_mid, doubles_full, preferred_element_type=f32)
    partial_density = jnp.einsum(
        "tae,tbe->ab",
        masked,
        lax.all_gather(amplitude_triples, "vir", axis=1, tiled=True),
        preferred_element_type=f32,
    )
    density = lax.psum(partial_density, "occ")
    density = (density / jnp.sqrt(f32(triples_all * width))).astype(jnp.bfloat16)
    density_term = jnp.einsum(
        "ac,tcb->tab",
        density,
        lax.all_gather(masked, "vir", axis=1, tiled=True),
        preferred_element_type=f32,
    )
    density_term = density_term / jnp.sqrt(f32(width))
    return (ladder_term + cycle_term + density_term).astype(jnp.bfloat16)


def solution(mesh):
    return jax.shard_map(
        on_device,
        mesh=mesh,
        in_specs=(
            P("occ", "vir", None),
            P("occ", "vir", None),
            P("occ"),
            P(None, "vir"),
            P(),
            P(None, "vir"),
        ),
        out_specs=P("occ", "vir", None),
        check_vma=False,
    )
```

profile of v0, /device:TPU:8, one launch (start us, length us, event | category | flops | bytes accessed | tf_op | source)
XLA Modules:
  0.0 227.4 jit_solution(11360172198900712387)
XLA Ops:
  6.5 0.0 copy-start
  6.5 0.0 copy-start.3
  6.5 0.0 copy-start.2
  6.5 0.0 all-gather.6.cloned.1.call-start
  6.5 0.7 all-gather.6.cloned.1.call-update
  7.3 0.0 all-gather.4.cloned.1.call-start
  7.3 0.7 iota_compare_fusion
  8.0 3.0 %broadcast_select_fusion = bf16[16,160,320]{2,1,0:T(8,128)(2,1)} fusion(bf16[16,160,320]{2,1,0:T(8,128)(2,1)} %param.6, pred[16,320]{1,0:T(8,128)(4,1)S(1)} %iota_compare_fusion), kind=kLoop, calls=%fused_computation.2 | loop fusion | flops 819200 | bytes 3281920 | tf_op jit(solution)/shard_map/jit(_where)/select_n | solution.py:15
  11.1 0.0 copy-start.1
  11.1 0.0 all-gather.4.cloned.1.call-update
  11.1 0.0 all-reduce.2.cloned.1.call-start
  11.2 0.0 copy-done.3
  11.2 4.6 %all-gather = bf16[2,160,40]{1,2,0:T(8,128)(2,1)S(1)} all-gather(bf16[1,160,40]{1,2,0:T(8,128)(2,1)S(1)} %bitcast.27), channel_id=1, replica_groups=mesh['occ'=16,'vir'=2] {'vir'}, dimensions={0}, use_global_device_ids=true | all-gather | bytes 38400 | tf_op jit(solution)/shard_map/all_gather | solution.py:18
  15.8 0.1 reshape.21
  15.9 0.0 copy-done.2
  15.9 6.4 %all_gather.12 = bf16[320,320]{0,1:T(8,128)(2,1)S(1)} all-gather(bf16[320,160]{0,1:T(8,128)(2,1)S(1)} %copy-done.2), channel_id=1, replica_groups=mesh['occ'=16,'vir'=2] {'vir'}, dimensions={1}, use_global_device_ids=true | all-gather | bytes 307200 | tf_op jit(solution)/shard_map/all_gather | solution.py:17
  22.3 4.9 %fusion.2 = f32[16,160,320]{2,1,0:T(8,128)} fusion(bf16[16,160,320]{2,1,0:T(8,128)(2,1)} %broadcast_select_fusion, bf16[320,320]{0,1:T(8,128)(2,1)S(1)} %all_gather.12), kind=kOutput, calls=%fused_computation.6 | convolution fusion | flops 524288000 | bytes 5120000 | tf_op jit(solution)/shard_map/tae,eb->tab/dot_general | solution.py:20
  27.2 36.7 %all-gather.6.cloned.1.call-done = bf16[16,320,320]{2,1,0:T(8,128)(2,1)} async-done(((bf16[16,160,320]{2,1,0:T(8,128)(2,1)}), bf16[16,320,320]{2,1,0:T(8,128)(2,1)}) %all-gather.6.cloned.1.call-update) | async-done | bytes 3276816 | tf_op jit(solution)/shard_map/all_gather | solution.py:28
  63.9 0.0 copy-done.1
  63.9 4.4 %convolution_bitcast_fusion = f32[160,320]{1,0:T(8,128)} fusion(bf16[16,160,320]{2,1,0:T(8,128)(2,1)S(1)} %copy-done.1, bf16[16,320,320]{2,1,0:T(8,128)(2,1)} %all-gather.6.cloned.1.call-done), kind=kOutput, calls=%fused_computation.5 | convolution fusion | flops 524288000 | bytes 5120000 | tf_op jit(solution)/shard_map/tae,tbe->ab/dot_general | solution.py:25
  68.3 0.0 all-reduce.2.cloned.1.call-update
  68.3 0.0 copy-done
  68.3 5.2 %fusion.1 = f32[16,160,320]{2,1,0:T(8,128)} fusion(bf16[320,40,1]{0,1,2:T(8,128)(2,1)S(1)} %reshape.21, bf16[16,160,320]{2,1,0:T(8,128)(2,1)} %param.7, bf16[320,40]{0,1:T(8,128)(2,1)S(1)} %copy-done), kind=kOutput, calls=%fused_computation.4 | convolution fusion | flops 131174400 | bytes 4966400 | tf_op jit(solution)/shard_map/tam,mb->tab/dot_general | solution.py:24
  73.5 46.9 %all-gather.4.cloned.1.call-done = bf16[16,320,320]{2,1,0:T(8,128)(2,1)} async-done(((bf16[16,160,320]{2,1,0:T(8,128)(2,1)}), bf16[16,320,320]{2,1,0:T(8,128)(2,1)}) %all-gather.4.cloned.1.call-update) | async-done | bytes 3276816 | tf_op jit(solution)/shard_map/all_gather | solution.py:36
  120.4 93.5 %all-reduce.2.cloned.1.call-done = f32[160,320]{1,0:T(8,128)} async-done(((f32[160,320]{1,0:T(8,128)}), f32[160,320]{1,0:T(8,128)}) %all-reduce.2.cloned.1.call-update) | async-done | bytes 204816 | tf_op jit(solution)/shard_map/psum | solution.py:31
  213.9 7.0 %fusion = bf16[16,160,320]{2,1,0:T(8,128)(2,1)} fusion(f32[16,160,320]{2,1,0:T(8,128)} %fusion.2, f32[16,160,320]{2,1,0:T(8,128)} %fusion.1, bf16[16,320,320]{2,1,0:T(8,128)(2,1)} %all-gather.4.cloned.1.call-done, f32[160,320]{1,0:T(8,128)} %all-reduce.2.cloned.1.call-done), kind=kOutput, calls=%fused_computation.1 | convolution fusion | flops 527667200 | bytes 11673600 | tf_op jit(solution)/shard_map/ac,tcb->tab/dot_general | solution.py:33
  (1 shorter events, 0.0 us)
Async XLA Ops:
  6.5 61.8 %copy-start = (bf16[320,40]{0,1:T(8,128)(2,1)S(1)}, bf16[320,40]{0,1:T(8,128)(2,1)}, u32[]{:S(2)}) copy-start(bf16[320,40]{0,1:T(8,128)(2,1)} %param.10) | copy-start | bytes 76804
  6.5 4.6 %copy-start.3 = (bf16[40,160]{1,0:T(8,128)(2,1)S(1)}, bf16[40,160]{1,0:T(8,128)(2,1)}, u32[]{:S(2)}) copy-start(bf16[40,160]{1,0:T(8,128)(2,1)} %param.11) | copy-start | bytes 38404
  6.5 9.4 %copy-start.2 = (bf16[320,160]{0,1:T(8,128)(2,1)S(1)}, bf16[320,160]{0,1:T(8,128)(2,1)}, u32[]{:S(2)}) copy-start(bf16[320,160]{0,1:T(8,128)(2,1)} %param.9) | copy-start | bytes 307204
  6.5 57.4 %all-gather.6.cloned.1.call-start = ((), (), s32[]{:S(2)}) async-start(), calls=%async_computation.1 | async-start | bytes 5898240 | tf_op jit(solution)/shard_map/all_gather | solution.py:28
  7.3 113.1 %all-gather.4.cloned.1.call-start = ((), (), s32[]{:S(2)}) async-start(), calls=%async_computation | async-start | bytes 5898240 | tf_op jit(solution)/shard_map/all_gather | solution.py:36
  11.1 52.8 %copy-start.1 = (bf16[16,160,320]{2,1,0:T(8,128)(2,1)S(1)}, bf16[16,160,320]{2,1,0:T(8,128)(2,1)}, u32[]{:S(2)}) copy-start(bf16[16,160,320]{2,1,0:T(8,128)(2,1)} %broadcast_select_fusion) | copy-start | bytes 4915204
  11.1 202.8 %all-reduce.2.cloned.1.call-start = ((), (), s32[]{:S(2)}) async-start(), calls=%async_computation.2 | async-start | bytes 491520 | tf_op jit(solution)/shard_map/psum | solution.py:31
Sparse Core Ops, SparseCore 0:
  8.9 54.9 all-gather.5
  65.4 54.8 all-gather.3
  123.8 90.0 all-reduce.1
where the time goes:
time: 228 us; the launch traced here: 227 us
  waiting for transfers between devices  178 us (78%)
  matrix products  21.4 us (9%)
  between operations  13.1 us (6%)
  blocking collectives  11 us (5%)
  other arithmetic  3.77 us (2%)
    psum x1, waiting for transfers between devices, on_device(): density = lax.psum(partial_density, 'occ')  93.5 us
    all_gather x1, waiting for transfers between devices, on_device(): lax.all_gather(masked, 'vir', axis=1, tiled=True)  46.9 us
    all_gather x1, waiting for transfers between devices, on_device(): lax.all_gather(amplitude_triples, 'vir', axis=1, tiled=True)  36.7 us
    dot_general x1, matrix products, on_device(): jnp.einsum('ac,tcb->tab', density, lax.all_gather(masked, 'vir', axis=1,...  6.97 us
    all_gather x1, blocking collectives, on_device(): lax.all_gather(ladder_weight, 'vir', axis=1, tiled=True)  6.43 us
    dot_general x1, matrix products, on_device(): jnp.einsum('tam,mb->tab', cycle_mid, doubles_full, preferred_element_type...  5.16 us
    dot_general x1, matrix products, on_device(): jnp.einsum('tae,eb->tab', masked, ladder_full, preferred_element_type=f32)  4.91 us
    all_gather x1, blocking collectives, on_device(): lax.all_gather(lambda_doubles, 'vir', axis=1, tiled=True)  4.59 us
  transfers between devices with their start and end apart: 3, of which 3 were waited for; matrix products, arithmetic and copies ran while one was open for 8% of the time, Pallas kernels for 0%

commit v1 on v0

--- a/solution.py
+++ b/solution.py
@@ -30,12 +30,27 @@
     )
     density = lax.psum(partial_density, "occ")
     density = (density / jnp.sqrt(f32(triples_all * width))).astype(jnp.bfloat16)
-    density_term = jnp.einsum(
+    size, position = (lax.axis_size("vir"), lax.axis_index("vir"))
+    left = [(i, (i - 1) % size) for i in range(size)]
+    rows = masked.shape[1]
+    held = masked
+    total = jnp.einsum(
         "ac,tcb->tab",
-        density,
-        lax.all_gather(masked, "vir", axis=1, tiled=True),
+        lax.dynamic_slice_in_dim(density, position * rows, held.shape[1], axis=1),
+        held,
         preferred_element_type=f32,
     )
+    for step in range(1, size):
+        held = lax.ppermute(held, "vir", left)
+        total = total + jnp.einsum(
+            "ac,tcb->tab",
+            lax.dynamic_slice_in_dim(
+                density, (position + step) % size * rows, held.shape[1], axis=1
+            ),
+            held,
+            preferred_element_type=f32,
+        )
+    density_term = total
     density_term = density_term / jnp.sqrt(f32(width))
     return (ladder_term + cycle_term + density_term).astype(jnp.bfloat16)
 

time: 228 us -> 212 us (0.930)
  waiting for transfers between devices: 178 us -> 87.9 us
  blocking collectives: 11 us -> 85.8 us
  matrix products: 21.4 us -> 18.8 us
    all_gather x1, blocking collectives: 4.59 us -> 77.3 us  [on_device(): lax.all_gather(lambda_doubles, 'vir', axis=1, tiled=True)]
    all_gather x1 -> x0, waiting for transfers between devices: 46.9 us -> none  [on_device(): lax.all_gather(masked, 'vir', axis=1, tiled=True)]
    all_gather x1, waiting for transfers between devices: 36.7 us -> 0.01 us  [on_device(): lax.all_gather(amplitude_triples, 'vir', axis=1, tiled=True)]
    psum x1, waiting for transfers between devices: 93.5 us -> 87.2 us  [on_device(): density = lax.psum(partial_density, 'occ')]
    dot_general x1 -> x2, matrix products: 6.97 us -> 6.12 us  [the longest x1 5.39 us: on_device(): jnp.einsum('ac,tcb->tab', lax.dynamic_slice_in_dim(density, (position + s...]
  transfers between devices with their start and end apart: 3 -> 3, of which waited for: 3 -> 1; matrix products, arithmetic and copies ran while one was open for 8% -> 8% of each run, Pallas kernels for 0% -> 0%
where the time goes in v1:
time: 212 us
  waiting for transfers between devices  87.9 us (41%)
  blocking collectives  85.8 us (40%)
  matrix products  18.8 us (9%)
  between operations  13.5 us (6%)
  other arithmetic  2.85 us (1%)
    psum x1, waiting for transfers between devices, on_device(): density = lax.psum(partial_density, 'occ')  87.2 us
    all_gather x1, blocking collectives, on_device(): lax.all_gather(lambda_doubles, 'vir', axis=1, tiled=True)  77.3 us
    all_gather x1, blocking collectives, on_device(): lax.all_gather(ladder_weight, 'vir', axis=1, tiled=True)  8.54 us
    dot_general x1, matrix products, on_device(): jnp.einsum('ac,tcb->tab', lax.dynamic_slice_in_dim(density, (position + s...  5.39 us
    dot_general x1, matrix products, on_device(): jnp.einsum('tam,mb->tab', cycle_mid, doubles_full, preferred_element_type...  5.07 us
    dot_general x1, matrix products, on_device(): jnp.einsum('tae,tbe->ab', masked, lax.all_gather(amplitude_triples, 'vir'...  4.42 us
  transfers between devices with their start and end apart: 3, of which 1 were waited for; matrix products, arithmetic and copies ran while one was open for 8% of the time, Pallas kernels for 0%

profile of v1, /device:TPU:8, one launch (start us, length us, event | category | flops | bytes accessed | tf_op | source)
XLA Modules:
  0.0 212.0 jit_solution(5111556831285195092)
XLA Ops:
  6.5 0.0 copy-start
  6.5 0.0 copy-start.4
  6.5 0.0 all-gather.3.cloned.1.call-start
  6.5 0.7 all-gather.3.cloned.1.call-update
  7.3 0.0 all-reduce.2.cloned.1.call-start
  7.3 0.0 copy-done.4
  7.3 0.1 iota_compare_fusion
  7.4 0.0 copy-start.3
  7.4 0.0 copy-start.2
  7.4 1.8 broadcast_select_fusion
  9.2 1.6 collective-permute-start
  10.8 0.0 copy-done.3
  10.8 77.3 %all-gather = bf16[2,160,40]{1,2,0:T(8,128)(2,1)S(1)} all-gather(bf16[1,160,40]{1,2,0:T(8,128)(2,1)S(1)} %bitcast.31), channel_id=1, replica_groups=mesh['occ'=16,'vir'=2] {'vir'}, dimensions={0}, use_global_device_ids=true | all-gather | bytes 38400 | tf_op jit(solution)/shard_map/all_gather | solution.py:18
  88.1 0.1 reshape.21
  88.2 0.0 copy-done.2
  88.2 8.5 %all_gather.9 = bf16[320,320]{0,1:T(8,128)(2,1)S(1)} all-gather(bf16[320,160]{0,1:T(8,128)(2,1)S(1)} %copy-done.2), channel_id=1, replica_groups=mesh['occ'=16,'vir'=2] {'vir'}, dimensions={1}, use_global_device_ids=true | all-gather | bytes 307200 | tf_op jit(solution)/shard_map/all_gather | solution.py:17
  96.8 3.2 %fusion.2 = f32[16,160,320]{2,1,0:T(8,128)} fusion(bf16[16,160,320]{2,1,0:T(8,128)(2,1)S(1)} %broadcast_select_fusion, bf16[320,320]{0,1:T(8,128)(2,1)S(1)} %all_gather.9), kind=kOutput, calls=%fused_computation.6 | convolution fusion | flops 524288000 | bytes 5120000 | tf_op jit(solution)/shard_map/tae,eb->tab/dot_general | solution.py:20
  100.0 0.0 all-gather.3.cloned.1.call-done
  100.0 4.4 %convolution_bitcast_fusion = f32[160,320]{1,0:T(8,128)} fusion(bf16[16,160,320]{2,1,0:T(8,128)(2,1)S(1)} %broadcast_select_fusion, bf16[16,320,320]{2,1,0:T(8,128)(2,1)} %all-gather.3.cloned.1.call-done), kind=kOutput, calls=%fused_computation.5 | convolution fusion | flops 524288000 | bytes 5120000 | tf_op jit(solution)/shard_map/tae,tbe->ab/dot_general | solution.py:25
  104.4 0.0 all-reduce.2.cloned.1.call-update
  104.4 0.0 copy-done
  104.4 5.1 %fusion.1 = f32[16,160,320]{2,1,0:T(8,128)} fusion(bf16[320,40,1]{0,1,2:T(8,128)(2,1)S(1)} %reshape.21, bf16[16,160,320]{2,1,0:T(8,128)(2,1)} %param.7, bf16[320,40]{0,1:T(8,128)(2,1)S(1)} %copy-done), kind=kOutput, calls=%fused_computation.4 | convolution fusion | flops 131174400 | bytes 4966400 | tf_op jit(solution)/shard_map/tam,mb->tab/dot_general | solution.py:24
  109.5 87.2 %all-reduce.2.cloned.1.call-done = f32[160,320]{1,0:T(8,128)} async-done(((f32[160,320]{1,0:T(8,128)}), f32[160,320]{1,0:T(8,128)}) %all-reduce.2.cloned.1.call-update) | async-done | bytes 204816 | tf_op jit(solution)/shard_map/psum | solution.py:31
  196.7 1.0 multiply_convert_fusion
  197.6 0.0 copy-start.1
  197.6 0.7 fusion.5
  198.4 0.0 collective-permute-done
  198.4 1.4 copy-done.1
  199.7 5.4 %fusion = bf16[16,160,320]{2,1,0:T(8,128)(2,1)} fusion(f32[16,320,160]{1,2,0:T(8,128)S(1)} %fusion.5, f32[16,160,320]{2,1,0:T(8,128)} %fusion.2, f32[16,160,320]{2,1,0:T(8,128)S(1)} %copy-done.1, bf16[16,160,320]{2,1,0:T(8,128)(2,1)} %collective-permute-done, bf16[160,320]{1,0:T(8,128)(2,1)S(1)} %multiply_convert_fusion, s32[]{:T(128)S(6)} %select_n.20), kind=kOutput, calls=%fused_computation.1 | convolution fusion | flops 266240000 | bytes 14499844 | tf_op jit(solution)/shard_map/ac,tcb->tab/dot_general | solution.py:45
  (1 shorter events, 0.0 us)
Async XLA Ops:
  6.5 97.9 %copy-start = (bf16[320,40]{0,1:T(8,128)(2,1)S(1)}, bf16[320,40]{0,1:T(8,128)(2,1)}, u32[]{:S(2)}) copy-start(bf16[320,40]{0,1:T(8,128)(2,1)} %param.10) | copy-start | bytes 76804
  6.5 0.8 copy-start.4
  6.5 93.4 %all-gather.3.cloned.1.call-start = ((), (), s32[]{:S(2)}) async-start(), calls=%async_computation | async-start | bytes 5898240 | tf_op jit(solution)/shard_map/all_gather | solution.py:28
  7.3 189.4 %all-reduce.2.cloned.1.call-start = ((), (), s32[]{:S(2)}) async-start(), calls=%async_computation.1 | async-start | bytes 491520 | tf_op jit(solution)/shard_map/psum | solution.py:31
  7.4 3.4 %copy-start.3 = (bf16[40,160]{1,0:T(8,128)(2,1)S(1)}, bf16[40,160]{1,0:T(8,128)(2,1)}, u32[]{:S(2)}) copy-start(bf16[40,160]{1,0:T(8,128)(2,1)} %param.11) | copy-start | bytes 38404
  7.4 80.8 %copy-start.2 = (bf16[320,160]{0,1:T(8,128)(2,1)S(1)}, bf16[320,160]{0,1:T(8,128)(2,1)}, u32[]{:S(2)}) copy-start(bf16[320,160]{0,1:T(8,128)(2,1)} %param.9) | copy-start | bytes 307204
  9.2 189.1 %collective-permute-start = (bf16[16,160,320]{2,1,0:T(8,128)(2,1)S(1)}, bf16[16,160,320]{2,1,0:T(8,128)(2,1)}, u32[]{:S(2)}, u32[]{:S(2)}) collective-permute-start(bf16[16,160,320]{2,1,0:T(8,128)(2,1)S(1)} %broadcast_select_fusion), channel_id=1, source_target_pairs={{0,1},{1,0},{2,3},{3,2},{4,5},{5,4},{6,7},{7,6},{8,9},{9,8},{10,11... | collective-permute-start | bytes 4915208 | tf_op jit(solution)/shard_map/ppermute | solution.py:44
  197.6 2.1 copy-start.1
Sparse Core Ops, SparseCore 0:
  8.9 90.3 all-gather.2
  104.5 92.0 all-reduce.1
